TPU v7x, 32 devices: a whole 2x2x4 slice. The times are simulated.
32 devices in a mesh: ob: 8 (over z, core), pt: 4 (over y, x).
Axes of the slice: x: 2, y: 2, z: 4, core: 2. Of those that a mesh axis runs over, the one named last changes fastest.
Arguments:
- orbitals: float32 [128, 262144], P(('ob', 'pt')), may hold values from -32 to 32, as said below
- potential: float32 [262144], replicated, may hold values from 0 to 2
- cutoff: float32 [1], replicated, may hold values from 0.4 to 1
- eigvec: float32 [128, 128], replicated, may hold values from -3 to 3, as said below
Outputs:
- gram: float32 [128, 128], P(('ob', 'pt'))
- hamil_sub: float32 [128, 128], P(('ob', 'pt'))
- rotated: float32 [128, 262144], P(None, ('ob', 'pt'))
- residual: float32 [128, 262144], P(None, ('ob', 'pt'))
- ritz: float32 [128], replicated
Inputs may be any that keep to these rules, and one draw needn't show every extreme that they name: `orbitals`: each orbital is a rough field whose scale differs from orbital to orbital and from region to region of the grid. `eigvec`: A full-rank matrix with a unit-sized diagonal and independent off-diagonal entries.
All inputs are finite; a program needn't handle non-finite values.
Results may differ from a plain program's by a relative error of at most 0.00027.
Values sent between devices are 32-bit elements; how exact they have to be, the bound alone decides.
A program may use at most 128 MiB of HBM per device.

v0:
```python
import functools

import jax
import jax.numpy as jnp
from jax import lax
from jax.experimental import pallas as pl
from jax.experimental.pallas import tpu as pltpu
from jax.sharding import PartitionSpec as P

G = 64
DEGREE = 12
LANES = 128
UNROLL = 16
MESH = pl.DeviceIdType.MESH
upper_bound = 8.0
quot_eps = 1e-06


def shift_matrix():
    row = lax.broadcasted_iota(jnp.int32, (2 * LANES, 2 * LANES), 0) % LANES
    col = lax.broadcasted_iota(jnp.int32, (2 * LANES, 2 * LANES), 1)
    lane = col % LANES
    step = (row - lane) % G
    z_pair = (row // G == lane // G) & ((step == 1) | (step == G - 1))
    swap = (row + G) % LANES == lane
    return jnp.where(col < LANES, z_pair, swap).astype(jnp.bfloat16)


def split(x):
    hi = x.astype(jnp.bfloat16)
    return hi, (x - hi.astype(jnp.float32)).astype(jnp.bfloat16)


def row_masks():
    shape = (1, 8, LANES)
    high_lane = lax.broadcasted_iota(jnp.int32, shape, 2) >= G
    low_sub = lax.broadcasted_iota(jnp.int32, shape, 1) < 4
    return high_lane & ~low_sub, ~high_lane & low_sub


def neighbour_sum(v, x_lower, x_upper, masks, shifts):
    m_up, m_down = masks
    hi, lo = split(v.reshape(-1, LANES))
    both = jnp.dot(
        jnp.concatenate([hi, lo], axis=1), shifts, preferred_element_type=jnp.float32
    )
    z_pair = both[:, :LANES].reshape(v.shape)
    w = both[:, LANES:].reshape(v.shape)
    r = pltpu.roll(w, 4, 1)
    above = jnp.concatenate([r[1:], r[:1]], axis=0)
    below = jnp.concatenate([r[-1:], r[:-1]], axis=0)
    t = jnp.where(m_up, above, jnp.where(m_down, below, r))
    return (x_lower + x_upper) + (w + t) + z_pair


def run_filter(cut_ref, pot_ref, orb_ref, shift_ref, filt, spare, coef_ref, sem):
    plane = pot_ref.shape[0] // G
    cut = cut_ref[0]
    center = 0.5 * (upper_bound + cut)
    half_width = 0.5 * (upper_bound - cut)
    inv = 1.0 / half_width
    copy = pltpu.make_async_copy(orb_ref, filt, sem)
    copy.start()

    def prep(x, c):
        rows = pl.ds(x * plane, plane)
        coef_ref[rows] = (2.0 * inv) * (pot_ref[rows] + (3.0 - center))
        return c

    lax.fori_loop(0, G, prep, 0)
    copy.wait()
    masks = row_masks()

    def sweep(cur, dst, first):
        def one(x):
            here = pl.ds(x * plane, plane)
            down = pl.ds((x + G - 1) % G * plane, plane)
            up = pl.ds((x + 1) % G * plane, plane)
            v = cur[here]
            s = neighbour_sum(v, cur[down], cur[up], masks, shift_ref[...])
            g = coef_ref[here] * v - inv * s
            return here, 0.5 * g if first else g - dst[here]

        def body(i, c):
            for here, value in [one(i * UNROLL + u) for u in range(UNROLL)]:
                dst[here] = value
            return c

        lax.fori_loop(0, G // UNROLL, body, 0)

    sweep(filt, spare, True)

    def pair(j, c):
        sweep(spare, filt, False)
        sweep(filt, spare, False)
        return c

    lax.fori_loop(0, (DEGREE - 2) // 2, pair, 0)
    sweep(spare, filt, False)


def filter_kernel(n_ob, n_pt, cut_ref, pot_ref, orb_ref, shift_ref, filt_out, appl_out, ext, spare, coef_ref, zbuf, sem, zsend, zrecv, psend, precv, own_sem):
    blocks = pot_ref.shape[0]
    plane = blocks // G
    outer = n_ob // 2
    peers = 2 * n_pt
    slab = blocks // outer
    piece = slab // peers
    ob, pt = lax.axis_index("ob"), lax.axis_index("pt")
    group = ob // 2
    seat = ob % 2 * n_pt + pt

    def group_dev(d):
        return ((group + d) % outer * 2 + ob % 2, pt)

    def peer_dev(k):
        to = (seat + k) % peers
        return (group * 2 + to // n_pt, to % n_pt)

    barrier = pltpu.get_barrier_semaphore()
    for d in range(1, outer):
        pl.semaphore_signal(barrier, inc=1, device_id=group_dev(d), device_id_type=MESH)
    for k in range(1, peers):
        pl.semaphore_signal(barrier, inc=1, device_id=peer_dev(k), device_id_type=MESH)

    filt = ext.at[pl.ds(plane, blocks)]
    run_filter(cut_ref, pot_ref, orb_ref, shift_ref, filt, spare, coef_ref, sem)
    ext[pl.ds(0, plane)] = ext[pl.ds(blocks, plane)]
    ext[pl.ds(plane + blocks, plane)] = ext[pl.ds(plane, plane)]
    pl.semaphore_wait(barrier, outer + peers - 2)

    def zcopy(d):
        return pltpu.make_async_remote_copy(
            src_ref=ext.at[pl.ds((group + d) % outer * slab, slab + 2 * plane)],
            dst_ref=zbuf.at[d - 1],
            send_sem=zsend.at[d],
            recv_sem=zrecv.at[d],
            device_id=group_dev(d),
            device_id_type=MESH,
        )

    for d in range(1, outer):
        zcopy(d).start()
    masks = row_masks()
    unroll = min(8, slab // plane)

    def source(d):
        return ext.at[pl.ds(group * slab, slab + 2 * plane)] if d == 0 else zbuf.at[d - 1]

    def pcopies(d, k):
        to = (seat + k) % peers
        slot = (group + outer - d) % outer * peers + seat
        srcs = (
            source(d).at[pl.ds(plane + to * piece, piece)],
            spare.at[pl.ds(d * slab + to * piece, piece)],
        )
        return [
            pltpu.make_async_remote_copy(
                src_ref=srcs[i],
                dst_ref=out.at[slot],
                send_sem=psend.at[d, k, i],
                recv_sem=precv.at[d, k, i],
                device_id=peer_dev(k),
                device_id_type=MESH,
            )
            for i, out in enumerate((filt_out, appl_out))
        ]

    def own_copies(d):
        slot = (group + outer - d) % outer * peers + seat
        srcs = (
            source(d).at[pl.ds(plane + seat * piece, piece)],
            spare.at[pl.ds(d * slab + seat * piece, piece)],
        )
        return [
            pltpu.make_async_copy(srcs[i], out.at[slot], own_sem.at[d, i])
            for i, out in enumerate((filt_out, appl_out))
        ]

    def dispatch(d, i):
        def send(k, c):
            pcopies(d, k)[i].start()
            return c

        lax.fori_loop(1, peers, send, 0)
        own_copies(d)[i].start()

    for d in range(outer):
        if d > 0:
            zcopy(d).wait_recv()
        dispatch(d, 0)
        src = source(d)

        def body(i, c):
            for u in range(unroll):
                x = i * unroll + u
                v = src[pl.ds((x + 1) * plane, plane)]
                s = neighbour_sum(
                    v,
                    src[pl.ds(x * plane, plane)],
                    src[pl.ds((x + 2) * plane, plane)],
                    masks,
                    shift_ref[...],
                )
                rows = pl.ds(group * slab + x * plane, plane)
                spare[pl.ds(d * slab + x * plane, plane)] = (pot_ref[rows] + 3.0) * v - 0.5 * s
            return c

        lax.fori_loop(0, slab // plane // unroll, body, 0)

        dispatch(d, 1)

    for d in range(outer):

        def finish(k, c):
            for copy in pcopies(d, k):
                copy.wait()
            return c

        lax.fori_loop(1, peers, finish, 0)
        for copy in own_copies(d):
            copy.wait()
        if d > 0:
            zcopy(d).wait_send()


def chebyshev(flat, pot, cutoff, n_ob, n_pt):
    vmem = pl.BlockSpec(memory_space=pltpu.VMEM)
    anywhere = pl.BlockSpec(memory_space=pl.ANY)
    blocks = flat.shape[0]
    outer, peers, plane = n_ob // 2, 2 * n_pt, blocks // G
    slab = blocks // outer
    result = jax.ShapeDtypeStruct((n_ob * n_pt, slab // peers, 8, LANES), jnp.float32)
    dma = pltpu.SemaphoreType.DMA
    return pl.pallas_call(
        functools.partial(filter_kernel, n_ob, n_pt),
        out_shape=(result, result),
        in_specs=[pl.BlockSpec(memory_space=pltpu.SMEM), vmem, anywhere, vmem],
        out_specs=(anywhere, anywhere),
        scratch_shapes=[
            pltpu.VMEM((blocks + 2 * plane, 8, LANES), jnp.float32),
            pltpu.VMEM(flat.shape, jnp.float32),
            pltpu.VMEM(flat.shape, jnp.float32),
            pltpu.VMEM((outer - 1, slab + 2 * plane, 8, LANES), jnp.float32),
            dma,
            dma((outer,)),
            dma((outer,)),
            dma((outer, peers, 2)),
            dma((outer, peers, 2)),
            dma((outer, 2)),
        ],
        compiler_params=pltpu.CompilerParams(
            collective_id=0, has_side_effects=True, vmem_limit_bytes=48 * 2**20
        ),
        name="filter",
    )(cutoff, pot, flat, shift_matrix())


def dot3(a, b, contract):
    dims = ((contract[:1], contract[1:]), ((), ()))
    one = functools.partial(
        lax.dot_general, dimension_numbers=dims, preferred_element_type=jnp.float32
    )
    return one(a[0], b[0]) + (one(a[0], b[1]) + one(a[1], b[0]))


def rotate_kernel(eig_ref, filt_ref, appl_ref, rot_ref, rota_ref, gram_ref, hamil_ref, num_ref, den_ref):
    rows = num_ref.shape[0]

    @pl.when(pl.program_id(0) == 0)
    def _():
        gram_ref[...] = jnp.zeros_like(gram_ref)
        hamil_ref[...] = jnp.zeros_like(hamil_ref)
        num_ref[...] = jnp.zeros_like(num_ref)
        den_ref[...] = jnp.zeros_like(den_ref)

    eig = split(eig_ref[...])

    def body(b, c):
        f = split(filt_ref[:, b].reshape(2 * rows, LANES))
        a = split(appl_ref[:, b].reshape(2 * rows, LANES))
        gram_ref[...] += dot3(f, f, (1, 1))
        hamil_ref[...] += dot3(f, a, (1, 1))
        rot = dot3(eig, f, (1, 0))
        rota = dot3(eig, a, (1, 0))
        for par in range(2):
            cols = pl.ds(pl.multiple_of((2 * b + par) * LANES, LANES), LANES)
            x = rot[par * rows : (par + 1) * rows]
            y = rota[par * rows : (par + 1) * rows]
            rot_ref[:, cols] = x
            rota_ref[:, cols] = y
            num_ref[...] += x * y
            den_ref[...] += x * x
        return c

    lax.fori_loop(0, filt_ref.shape[1], body, 0)


def rotate(filt, appl, eigvec):
    rows = eigvec.shape[0]
    n_src, blocks = filt.shape[:2]
    per_dev = rows // n_src
    step = min(blocks, max(1, 8 * 128 // rows))
    parity = lax.broadcasted_iota(jnp.int32, (2 * rows, 1), 0) // per_dev % 2
    doubled = jnp.broadcast_to(
        eigvec.reshape(n_src, 1, per_dev, rows), (n_src, 2, per_dev, rows)
    ).reshape(2 * rows, rows)
    spread = jnp.concatenate(
        [jnp.where(parity == 0, doubled, 0.0), jnp.where(parity == 1, doubled, 0.0)], axis=1
    ).T
    f32 = lambda *s: jax.ShapeDtypeStruct(s, jnp.float32)
    whole = lambda *s: pl.BlockSpec(s, lambda i: (0,) * len(s))
    field = pl.BlockSpec((n_src, step, 8, LANES), lambda i: (0, i, 0, 0))
    out = pl.BlockSpec((rows, 2 * step * LANES), lambda i: (0, i))
    rot, rota, gram, hamil, num, den = pl.pallas_call(
        rotate_kernel,
        grid=(blocks // step,),
        out_shape=(
            f32(rows, 2 * blocks * LANES),
            f32(rows, 2 * blocks * LANES),
            f32(2 * rows, 2 * rows),
            f32(2 * rows, 2 * rows),
            f32(rows, LANES),
            f32(rows, LANES),
        ),
        in_specs=[whole(2 * rows, 2 * rows), field, field],
        out_specs=(
            out,
            out,
            whole(2 * rows, 2 * rows),
            whole(2 * rows, 2 * rows),
            whole(rows, LANES),
            whole(rows, LANES),
        ),
        compiler_params=pltpu.CompilerParams(vmem_limit_bytes=56 * 2**20),
        name="rotate",
    )(spread, filt, appl)

    def fold(m):
        m = jnp.where(parity == parity.T, m, 0.0)
        half = m.reshape(n_src, 2, per_dev, 2 * rows).sum(axis=1).reshape(rows, 2 * rows).T
        return half.reshape(n_src, 2, per_dev, rows).sum(axis=1).reshape(rows, rows).T

    return rot, rota, fold(gram), fold(hamil), num.sum(axis=1), den.sum(axis=1)


def reduce_kernel(n_ob, n_pt, part_ref, out_ref, recv, send_sem, recv_sem):
    n_dev = n_ob * n_pt
    me = lax.axis_index("ob") * n_pt + lax.axis_index("pt")
    barrier = pltpu.get_barrier_semaphore()

    def copy(k):
        to = (me + k) % n_dev
        return pltpu.make_async_remote_copy(
            src_ref=part_ref.at[to],
            dst_ref=recv.at[k],
            send_sem=send_sem.at[k],
            recv_sem=recv_sem.at[k],
            device_id=(to // n_pt, to % n_pt),
            device_id_type=MESH,
        )

    def greet(k, c):
        to = (me + k) % n_dev
        pl.semaphore_signal(
            barrier, inc=1, device_id=(to // n_pt, to % n_pt), device_id_type=MESH
        )
        return c

    def start(k, c):
        copy(k).start()
        return c

    def finish(k, total):
        copy(k).wait()
        return total + recv[k]

    lax.fori_loop(1, n_dev, greet, 0)
    pl.semaphore_wait(barrier, n_dev - 1)
    lax.fori_loop(1, n_dev, start, 0)
    out_ref[...] = lax.fori_loop(1, n_dev, finish, part_ref[me])


def reduce_parts(parts, n_ob, n_pt):
    n_dev, rows, cols = parts.shape
    vmem = pl.BlockSpec(memory_space=pltpu.VMEM)
    return pl.pallas_call(
        functools.partial(reduce_kernel, n_ob, n_pt),
        out_shape=jax.ShapeDtypeStruct((rows, cols), jnp.float32),
        in_specs=[vmem],
        out_specs=vmem,
        scratch_shapes=[
            pltpu.VMEM((n_dev, rows, cols), jnp.float32),
            pltpu.SemaphoreType.DMA((n_dev,)),
            pltpu.SemaphoreType.DMA((n_dev,)),
        ],
        compiler_params=pltpu.CompilerParams(
            collective_id=1, has_side_effects=True, vmem_limit_bytes=32 * 2**20
        ),
        name="reduce_parts",
    )(parts)


def on_device(orbitals, potential, cutoff, eigvec):
    axes = ("ob", "pt")
    total_orb = eigvec.shape[0]
    n_ob, n_pt = lax.axis_size("ob"), lax.axis_size("pt")
    n_dev = n_ob * n_pt
    per_dev, npts = orbitals.shape
    tiles = npts // LANES
    flat = orbitals.reshape(per_dev, tiles, LANES).transpose(1, 0, 2).reshape(-1, 8, LANES)
    pot = jnp.broadcast_to(
        potential.reshape(tiles, 1, LANES), (tiles, per_dev, LANES)
    ).reshape(-1, 8, LANES)
    filtered, applied = chebyshev(flat, pot, cutoff, n_ob, n_pt)
    rotated, rot_applied, gram, hamil, numer, denom = rotate(filtered, applied, eigvec)
    quotient = jnp.broadcast_to(jnp.stack([numer, denom]), (n_dev, 2, total_orb))
    parts = jnp.concatenate(
        [
            gram.reshape(n_dev, per_dev, total_orb),
            hamil.reshape(n_dev, per_dev, total_orb),
            quotient,
            jnp.zeros((n_dev, -(2 * per_dev + 2) % 8, total_orb), jnp.float32),
        ],
        axis=1,
    )
    sums = reduce_parts(parts, n_ob, n_pt) / npts
    gram, hamil_sub = sums[:per_dev], sums[per_dev : 2 * per_dev]
    numer, denom = sums[2 * per_dev], sums[2 * per_dev + 1]
    ritz = numer / (denom + quot_eps)
    residual = rot_applied - ritz[:, None] * rotated
    return (gram, hamil_sub, rotated, residual, ritz)


def solution(mesh):
    return jax.shard_map(
        on_device,
        mesh=mesh,
        in_specs=(P(("ob", "pt"), None), P(), P(), P()),
        out_specs=(
            P(("ob", "pt"), None),
            P(("ob", "pt"), None),
            P(None, ("ob", "pt")),
            P(None, ("ob", "pt")),
            P(),
        ),
        check_vma=False,
    )
```

profile of v0, /device:TPU:0, one launch (start us, length us, event | category | flops | bytes accessed | tf_op | source)
XLA Modules:
  0.0 237.0 jit_solution(6868331806806824318)
XLA Ops:
  0.6 0.9 broadcast_in_dim.46
  1.5 0.1 copy.16
  1.6 0.7 maximum_bitcast_fusion.eig_ref
  2.4 0.4 fusion.21.shift_ref
  2.8 3.4 %broadcast_in_dim.50 = f32[2048,4,128]{2,1,0:T(4,128)} broadcast(f32[2048,128]{1,0:T(8,128)} %bitcast.29), dimensions={0,2} | broadcast | bytes 5242880 | tf_op jit(solution)/shard_map/broadcast_in_dim | solution.py:412
  6.9 163.5 %filter.1 = (f32[32,32,8,128]{3,2,1,0:T(8,128)S(1)}, f32[32,32,8,128]{3,2,1,0:T(8,128)}) custom-call(f32[1]{0:T(128)S(6)} %copy.23.cut_ref, f32[1024,8,128]{2,1,0:T(8,128)} %bitcast.27, f32[1024,8,128]{2,1,0:T(8,128)} %bitcast.28, bf16[256,256]{1,0:T(8,128)(2,1)S(1)} %fusion.21.shift_ref), custom_call_target="tpu_custom_call" | custom-call | tf_op jit(solution)/shard_map/filter/pallas_call | solution.py:235
  170.4 2.0 copy-done
  172.4 22.1 %rotate.1 = (f32[128,8192]{1,0:T(8,128)}, f32[128,8192]{1,0:T(8,128)}, f32[256,256]{1,0:T(8,128)}, f32[256,256]{1,0:T(8,128)}, f32[128,128]{1,0:T(8,128)}, /*index=5*/f32[128,128]{1,0:T(8,128)}) custom-call(f32[256,256]{1,0:T(8,128)} %maximum_bitcast_fusion.eig_ref, f32[32,32,8,128]{3,2,1,0:T(8,128)} %copy-done, f32[32,32,8,128]{3,2,1,0:T(8,128)} %get-tuple-element.14.appl_ref), custom_call_target="tpu_custom_call" | custom-call | tf_op jit(solution)/shard_map/rotate/pallas_call | solution.py:315
  194.5 1.2 compare_select_fusion.1
  195.6 0.1 reshape.157
  195.7 0.1 reduce_sum.54
  195.9 0.1 copy.19
  196.0 0.1 copy.20
  196.1 0.1 reshape.162
  196.2 0.1 reduce_sum.56
  196.3 0.1 copy.21
  196.4 0.1 copy.22
  196.6 0.1 reduce_sum.58
  196.7 0.1 reduce_sum.59
  196.8 0.1 pad.3.clone
  196.9 0.1 maximum_maximum_fusion.part_ref
  197.0 33.2 %reduce_parts.1 = f32[16,128]{1,0:T(8,128)S(1)} custom-call(f32[32,16,128]{2,1,0:T(8,128)S(1)} %maximum_maximum_fusion.part_ref), custom_call_target="tpu_custom_call" | custom-call | tf_op jit(solution)/shard_map/reduce_parts/pallas_call | solution.py:387
  230.3 6.1 %multiply_subtract_fusion = f32[128,8192]{1,0:T(8,128)} fusion(f32[128,8192]{1,0:T(8,128)} %get-tuple-element.20, f32[128,8192]{1,0:T(8,128)} %get-tuple-element.10, f32[128]{0:T(128)S(1)} %fusion.25), kind=kLoop, calls=%fused_computation | loop fusion | flops 2097152 | bytes 12583424 | tf_op jit(solution)/shard_map/sub | solution.py:431
  236.4 0.6 fusion.26
  (21 shorter events, 0.3 us)
Async XLA Ops:
  170.3 2.0 copy-start
  194.4 2.1 copy-start.2
  194.5 2.2 copy-start.1
  230.2 6.1 %copy-start.3 = (f32[128]{0:T(128)}, f32[128]{0:T(128)S(1)}, u32[]{:S(2)}) copy-start(f32[128]{0:T(128)S(1)} %fusion.25) | copy-start | bytes 1540
where the time goes:
time: 238 us; the launch traced here: 237 us
  Pallas kernels  219 us (92%)
  other arithmetic  8.99 us (4%)
  local copies, waits for them, and re-layouts  7.67 us (3%)
    pallas_call x1, Pallas kernels, chebyshev(): pl.pallas_call(functools.partial(filter_kernel, n_ob, n_pt), out_shape=(r...  163 us
    pallas_call x1, Pallas kernels, reduce_parts(): pl.pallas_call(functools.partial(reduce_kernel, n_ob, n_pt), out_shape=ja...  33.2 us
    pallas_call x1, Pallas kernels, rotate(): pl.pallas_call(rotate_kernel, grid=(blocks // step,), out_shape=(f32(rows...  22.1 us
    sub x1, other arithmetic, on_device(): residual = rot_applied - ritz[:, None] * rotated  6.13 us

commit v1 on v0

v1 whole, which is shorter than its diff:
```python
import functools

import jax
import jax.numpy as jnp
from jax import lax
from jax.experimental import pallas as pl
from jax.experimental.pallas import tpu as pltpu
from jax.sharding import PartitionSpec as P

G = 64
DEGREE = 12
LANES = 128
SUBS = 8
ROWS = G * G // LANES
BLK = ROWS // SUBS
CHUNK = 16
MESH = pl.DeviceIdType.MESH
upper_bound = 8.0
quot_eps = 1e-06


def split(x):
    hi = x.astype(jnp.bfloat16)
    return hi, (x - hi.astype(jnp.float32)).astype(jnp.bfloat16)


def shift_matrix():
    row = lax.broadcasted_iota(jnp.int32, (2 * LANES, 2 * LANES), 0) % LANES
    col = lax.broadcasted_iota(jnp.int32, (2 * LANES, 2 * LANES), 1)
    lane = col % LANES
    step = (row - lane) % G
    z_pair = (row // G == lane // G) & ((step == 1) | (step == G - 1))
    swap = (row + G) % LANES == lane
    both = jnp.where(swap, 1.0, 0.0) + jnp.where((col < LANES) & z_pair, 1.0, 0.0)
    return both.astype(jnp.bfloat16)


def lateral(v, shifts):
    hi, lo = split(v.reshape(-1, LANES))
    both = jnp.dot(
        jnp.concatenate([hi, lo], axis=1), shifts, preferred_element_type=jnp.float32
    )
    near = both[:, :LANES].reshape(v.shape)
    w = both[:, LANES:].reshape(v.shape)
    below = jnp.concatenate([pltpu.roll(w[:, BLK - 1 :], 1, 2), w[:, : BLK - 1]], axis=1)
    above = jnp.concatenate([w[:, 1:], pltpu.roll(w[:, :1], SUBS - 1, 2)], axis=1)
    low = lax.broadcasted_iota(jnp.int32, (1, 1, 1, LANES), 3) < G
    return near + jnp.where(low, below, above)


def kernel(
    n_ob, n_pt,
    cut_ref, pot_hbm, orb_hbm, eig_ref,
    gram_out, hamil_out, ritz_out, rot_hbm, res_hbm,
    ext, spare, coef, pot, shifts, zbuf, appl, filt_all, appl_all, est, rot, rota,
    quot, quot_in, part, part_in,
    load_sem, pot_sem, zsend, zrecv, psend, precv, qsend, qrecv, gsend, grecv, out_sem,
):
    waves = ext.shape[0]
    outer, peers, n_dev = n_ob // 2, 2 * n_pt, n_ob * n_pt
    norb = eig_ref.shape[1]
    ppl = G // outer
    n_plane, _, n_sub = filt_all.shape[:3]
    per_plane = SUBS // n_sub
    npts = G * G * G
    ob, pt = lax.axis_index("ob"), lax.axis_index("pt")
    me = ob * n_pt + pt
    group = ob // 2
    seat = ob % 2 * n_pt + pt

    def device(i):
        return (i // n_pt, i % n_pt)

    half = group // max(1, outer // 2)
    mirrored = half * (outer - 1 - group) + (1 - half) * group

    def other_group(i):
        t = outer - 1 - i - (i + mirrored + 1) // outer
        return half * (outer - 1 - t) + (1 - half) * t

    barrier = pltpu.get_barrier_semaphore()

    def greet(k, c):
        pl.semaphore_signal(
            barrier, inc=1, device_id=device((me + k) % n_dev), device_id_type=MESH
        )
        return c

    def load(w, b):
        return pltpu.make_async_copy(
            orb_hbm.at[:, :, b * waves + w, :], ext.at[w, pl.ds(1, G), b], load_sem.at[w, b]
        )

    def load_pot(b):
        return pltpu.make_async_copy(pot_hbm.at[:, :, b, :], pot.at[:, b], pot_sem.at[b])

    for b in range(BLK):
        load(0, b).start()
    for b in range(BLK):
        load_pot(b).start()
    for w in range(1, waves):
        for b in range(BLK):
            load(w, b).start()
    lax.fori_loop(1, n_dev, greet, 0)

    cut = cut_ref[0]
    center = 0.5 * (upper_bound + cut)
    half_width = 0.5 * (upper_bound - cut)
    inv = 1.0 / half_width
    shifts[...] = shift_matrix()
    for w in range(waves):
        hi, lo = split(eig_ref[pl.ds(w * n_dev, n_dev), :].T)
        est[w] = jnp.concatenate([hi, lo, hi], axis=1)
    for b in range(BLK):
        load_pot(b).wait()

    def prep(x, c):
        coef[x] = (2.0 * inv) * (pot[x] + (3.0 - center))
        return c

    lax.fori_loop(0, G, prep, 0)

    def sweep(cur, dst, first):
        for q in range(G // CHUNK):
            lat = lateral(cur[pl.ds(q * CHUNK, CHUNK)], shifts[...])
            for u in range(CHUNK):
                x = q * CHUNK + u
                s = (cur[(x - 1) % G] + cur[(x + 1) % G]) + lat[u]
                g = coef[x] * cur[x] - inv * s
                dst[x] = 0.5 * g if first else g - dst[x]

    def zcopy(w, i):
        to = other_group(i)
        return pltpu.make_async_remote_copy(
            src_ref=ext.at[w, pl.ds(to * ppl, ppl + 2)],
            dst_ref=zbuf.at[group, w],
            send_sem=zsend.at[w, to],
            recv_sem=zrecv.at[w, group],
            device_id=(to * 2 + ob % 2, pt),
            device_id_type=MESH,
        )

    def zarrival(w, g):
        return pltpu.make_async_remote_copy(
            src_ref=zbuf.at[g, w],
            dst_ref=zbuf.at[g, w],
            send_sem=zsend.at[w, g],
            recv_sem=zrecv.at[w, g],
            device_id=(g * 2 + ob % 2, pt),
            device_id_type=MESH,
        )

    def piece(ref, first_plane, to):
        planes = pl.ds(first_plane + to // per_plane * n_plane, n_plane)
        if n_sub == SUBS:
            return ref.at[planes]
        return ref.at[planes, :, pl.ds(pl.multiple_of(to % per_plane * n_sub, n_sub), n_sub)]

    def dispatch(w, g, i):
        src, first = ((zbuf, 1), (appl, 0))[i]
        dst = (filt_all, appl_all)[i].at[:, :, :, w * n_dev + g * peers + seat, :]

        def send(k, c):
            to = (seat + k) % peers
            pltpu.make_async_remote_copy(
                src_ref=piece(src.at[g, w], first, to),
                dst_ref=dst,
                send_sem=psend.at[w, i],
                recv_sem=precv.at[w, i],
                device_id=(group * 2 + to // n_pt, to % n_pt),
                device_id_type=MESH,
            ).start()
            return c

        lax.fori_loop(1, peers, send, 0)
        pltpu.make_async_copy(piece(src.at[g, w], first, seat), dst, precv.at[w, i]).start()

    def process(w, g):
        dispatch(w, g, 0)
        src = zbuf.at[g, w]
        lat = lateral(src[pl.ds(1, ppl)], shifts[...])
        for x in range(ppl):
            s = (src[x] + src[x + 2]) + lat[x]
            appl[g, w, x] = (pot[group * ppl + x] + 3.0) * src[x + 1] - 0.5 * s
        dispatch(w, g, 1)

    def filter_wave(w, c):
        for b in range(BLK):
            load(w, b).wait()
        f = ext.at[w, pl.ds(1, G)]
        sweep(f, spare, True)

        def pair(j, c):
            sweep(spare, f, False)
            sweep(f, spare, False)
            return c

        lax.fori_loop(0, (DEGREE - 2) // 2, pair, 0)
        sweep(spare, f, False)
        ext[w, 0] = ext[w, G]
        ext[w, G + 1] = ext[w, 1]

        @pl.when(w == 0)
        def _():
            pl.semaphore_wait(barrier, n_dev - 1)

        for i in range(outer - 1):
            zcopy(w, i).start()
        zbuf[group, w] = ext[w, pl.ds(group * ppl, ppl + 2)]
        process(w, group)
        return c

    lax.fori_loop(0, waves, filter_wave, 0)

    def arrived(ref, w, sem):
        rows = ref.at[:, :, :, pl.ds(w * n_dev, n_dev), :]
        return pltpu.make_async_copy(rows, rows, sem)

    num = den = None

    def rotate(w):
        for i, ref in enumerate((filt_all, appl_all)):
            arrived(ref, w, precv.at[w, i]).wait()
        last = w == waves - 1
        rows = pl.ds(w * n_dev, n_dev)

        def body(t, c):
            p, b = t // BLK, t % BLK
            for h in range(n_sub // 2):
                pair = (2 * h, 2 * h + 1)
                f = jnp.concatenate(
                    [ref[p, b, s, rows, :] for ref in (filt_all, appl_all) for s in pair], axis=1
                )
                hi, lo = split(f)
                out = jnp.dot(
                    est[w], jnp.concatenate([hi, hi, lo], axis=0), preferred_element_type=jnp.float32
                )
                for j, s in enumerate(pair):
                    col = pl.ds(
                        pl.multiple_of((p * n_sub * BLK + s * BLK + b) * LANES, LANES), LANES
                    )
                    x = out[:, j * LANES : (j + 1) * LANES]
                    y = out[:, (2 + j) * LANES : (3 + j) * LANES]
                    if w > 0:
                        x += rot[:, col]
                        y += rota[:, col]
                    rot[:, col] = x
                    rota[:, col] = y
                    if last:
                        c = (c[0] + x * y, c[1] + x * x)
            return c

        zero = jnp.zeros((norb, LANES), jnp.float32)
        return lax.fori_loop(0, n_plane * BLK, body, (zero, zero) if last else 0)

    for w in range(waves):

        def arrival(i, c, w=w):
            g = other_group(i)
            zarrival(w, g).wait_recv()
            process(w, g)
            return c

        lax.fori_loop(0, outer - 1, arrival, 0)
        if w > 0:
            rotate(w - 1)
    num, den = rotate(waves - 1)

    out_rot = pltpu.make_async_copy(rot, rot_hbm, out_sem.at[0])
    out_rot.start()
    quot[...] = jnp.zeros_like(quot)
    quot[0, 0:1, :] = jnp.sum(num.T, axis=0, keepdims=True)
    quot[0, 1:2, :] = jnp.sum(den.T, axis=0, keepdims=True)

    def qcopy(k):
        return pltpu.make_async_remote_copy(
            src_ref=quot.at[0],
            dst_ref=quot_in.at[k],
            send_sem=qsend.at[k],
            recv_sem=qrecv.at[k],
            device_id=device((me + k) % n_dev),
            device_id_type=MESH,
        )

    def qstart(k, c):
        qcopy(k).start()
        return c

    lax.fori_loop(1, n_dev, qstart, 0)

    n_rows = n_plane * BLK

    def gram_body(t, c):
        p, b = t // BLK, t % BLK
        f = jnp.concatenate([filt_all[p, b, s] for s in range(n_sub)], axis=1)
        a = jnp.concatenate([appl_all[p, b, s] for s in range(n_sub)], axis=1)
        fh, fl = split(f)
        ah, al = split(a)
        nt = functools.partial(
            lax.dot_general,
            dimension_numbers=(((1,), (1,)), ((), ())),
            preferred_element_type=jnp.float32,
        )
        high = nt(jnp.concatenate([fh, fl], axis=0), jnp.concatenate([fh, ah], axis=0))
        low = nt(fh, jnp.concatenate([fl, al], axis=0))
        return c + (high[:norb] + (high[norb:] + low))

    both = lax.fori_loop(0, n_rows, gram_body, jnp.zeros((norb, 2 * norb), jnp.float32))
    for w in range(waves):
        rows = both[w * n_dev : (w + 1) * n_dev]
        part[:, w : w + 1, :] = rows[:, None, :norb]
        part[:, waves + w : waves + w + 1, :] = rows[:, None, norb:]

    def gcopy(k):
        to = (me + k) % n_dev
        return pltpu.make_async_remote_copy(
            src_ref=part.at[to],
            dst_ref=part_in.at[k],
            send_sem=gsend.at[k],
            recv_sem=grecv.at[k],
            device_id=device(to),
            device_id_type=MESH,
        )

    def gstart(k, c):
        gcopy(k).start()
        return c

    lax.fori_loop(1, n_dev, gstart, 0)

    def qfinish(k, total):
        qcopy(k).wait()
        return total + quot_in[k]

    total = lax.fori_loop(1, n_dev, qfinish, quot[0]) / npts
    ritz = total[0:1] / (total[1:2] + quot_eps)
    ritz_out[...] = ritz
    column = jnp.broadcast_to(ritz, (LANES, norb)).T

    n_cols = rot.shape[1] // LANES

    def residual(t, c):
        col = pl.ds(pl.multiple_of(t * LANES, LANES), LANES)
        rota[:, col] = rota[:, col] - column * rot[:, col]
        return c

    lax.fori_loop(0, n_cols, residual, 0)
    out_res = pltpu.make_async_copy(rota, res_hbm, out_sem.at[1])
    out_res.start()

    def gfinish(k, total):
        gcopy(k).wait()
        return total + part_in[k]

    sums = lax.fori_loop(1, n_dev, gfinish, part[me]) / npts
    gram_out[...] = sums[:waves]
    hamil_out[...] = sums[waves : 2 * waves]

    for w in range(waves):
        for i in range(outer - 1):
            zcopy(w, i).wait_send()
        share = n_dev * (peers - 1) // peers
        for i, ref in enumerate((filt_all, appl_all)):
            rows = ref.at[:, :, :, pl.ds(0, share), :]
            pltpu.make_async_copy(rows, rows, psend.at[w, i]).wait()
    out_rot.wait()
    out_res.wait()


def on_device(orbitals, potential, cutoff, eigvec):
    norb = eigvec.shape[0]
    n_ob, n_pt = lax.axis_size("ob"), lax.axis_size("pt")
    n_dev, outer = n_ob * n_pt, n_ob // 2
    waves, npts = orbitals.shape
    tiles = npts // LANES
    ppl = G // outer
    rows = tiles // n_dev
    n_plane, n_sub = max(1, rows // ROWS), min(SUBS, rows // BLK)
    orb = orbitals.reshape(waves, tiles, LANES).transpose(1, 0, 2)
    orb = orb.reshape(G, SUBS, BLK * waves, LANES)
    pot = potential.reshape(G, SUBS, BLK, LANES)
    eig = eigvec.reshape(n_dev, waves, norb).transpose(1, 0, 2).reshape(norb, norb)
    f32 = lambda *s: jax.ShapeDtypeStruct(s, jnp.float32)
    vm = lambda *s: pltpu.VMEM(s, jnp.float32)
    dma = pltpu.SemaphoreType.DMA
    vmem = pl.BlockSpec(memory_space=pltpu.VMEM)
    anywhere = pl.BlockSpec(memory_space=pl.ANY)
    padded = -(-2 * waves // SUBS) * SUBS
    gram, hamil, ritz, rotated, residual = pl.pallas_call(
        functools.partial(kernel, n_ob, n_pt),
        out_shape=(
            f32(waves, norb), f32(waves, norb), f32(1, norb),
            f32(norb, rows * LANES), f32(norb, rows * LANES),
        ),
        in_specs=[pl.BlockSpec(memory_space=pltpu.SMEM), anywhere, anywhere, vmem],
        out_specs=(vmem, vmem, vmem, anywhere, anywhere),
        scratch_shapes=[
            vm(waves, G + 2, BLK, SUBS, LANES),
            vm(G, BLK, SUBS, LANES),
            vm(G, BLK, SUBS, LANES),
            vm(G, BLK, SUBS, LANES),
            pltpu.VMEM((2 * LANES, 2 * LANES), jnp.bfloat16),
            vm(outer, waves, ppl + 2, BLK, SUBS, LANES),
            vm(outer, waves, ppl, BLK, SUBS, LANES),
            vm(n_plane, BLK, n_sub, norb, LANES),
            vm(n_plane, BLK, n_sub, norb, LANES),
            pltpu.VMEM((waves, norb, 3 * n_dev), jnp.bfloat16),
            vm(norb, rows * LANES),
            vm(norb, rows * LANES),
            vm(1, SUBS, norb),
            vm(n_dev, SUBS, norb),
            vm(n_dev, padded, norb),
            vm(n_dev, padded, norb),
            dma((waves, BLK)), dma((BLK,)),
            dma((waves, outer)), dma((waves, outer)),
            dma((waves, 2)), dma((waves, 2)),
            dma((n_dev,)), dma((n_dev,)), dma((n_dev,)), dma((n_dev,)),
            dma((2,)),
        ],
        compiler_params=pltpu.CompilerParams(
            collective_id=0, has_side_effects=True, vmem_limit_bytes=60 * 2**20
        ),
        name="filter_rotate",
    )(cutoff, pot, orb, eig)
    back = lambda m: m.reshape(waves, waves, n_dev).transpose(0, 2, 1).reshape(waves, norb)
    return (back(gram), back(hamil), rotated, residual, ritz[0])


def solution(mesh):
    return jax.shard_map(
        on_device,
        mesh=mesh,
        in_specs=(P(("ob", "pt"), None), P(), P(), P()),
        out_specs=(
            P(("ob", "pt"), None),
            P(("ob", "pt"), None),
            P(None, ("ob", "pt")),
            P(None, ("ob", "pt")),
            P(),
        ),
        check_vma=False,
    )
```

time: 238 us -> 165 us (0.69)
  Pallas kernels: 219 us -> 152 us
  other arithmetic: 8.99 us -> 0 us
  local copies, waits for them, and re-layouts: 7.67 us -> 11.9 us
    pallas_call x3 -> x1, Pallas kernels: 219 us -> 152 us  [on_device(): pl.pallas_call(functools.partial(kernel, n_ob, n_pt), out_shape=(f32(wave...]
    sub x1 -> x0, other arithmetic: 6.13 us -> none  [on_device(): residual = rot_applied - ritz[:, None] * rotated]
    unnamed x8 -> x7, local copies, waits for them, and re-layouts: 2.02 us -> 7.29 us
    broadcast_in_dim x4 -> x0, local copies, waits for them, and re-layouts: 4.3 us -> none  [the longest x1 3.42 us: on_device(): jnp.broadcast_to(potential.reshape(tiles, 1, LANES), (tiles, per_dev, LAN...]
    reshape x5 -> x7, local copies, waits for them, and re-layouts: 0.34 us -> 4.57 us  [the longest x6 3.09 us: on_device(): m.reshape(waves, waves, n_dev).transpose(0, 2, 1).reshape(waves, norb)]
where the time goes in v1:
time: 165 us
  Pallas kernels  152 us (92%)
  local copies, waits for them, and re-layouts  11.9 us (7%)
    pallas_call x1, Pallas kernels, on_device(): pl.pallas_call(functools.partial(kernel, n_ob, n_pt), out_shape=(f32(wave...  152 us
    unnamed x7, local copies, waits for them, and re-layouts  7.29 us

profile of v1, /device:TPU:0, one launch (start us, length us, event | category | flops | bytes accessed | tf_op | source)
XLA Modules:
  0.0 165.1 jit_solution(2206800957755966909)
XLA Ops:
  1.3 1.5 copy.14
  2.8 151.9 %filter_rotate.1 = (f32[4,128]{1,0:T(4,128)}, f32[4,128]{1,0:T(4,128)}, f32[1,128]{1,0:T(1,128)}, f32[128,8192]{1,0:T(8,128)}, f32[128,8192]{1,0:T(8,128)}) custom-call(f32[1]{0:T(128)S(6)} %copy.20.cut_ref, f32[64,8,4,128]{3,2,1,0:T(4,128)} %bitcast.14, f32[64,8,16,128]{3,2,1,0:T(8,128)} %bitcast.13, f32[128,128]{1,0:T(8,128)} %bitcast.15), custom_call_target="tpu_custom_call" | custom-call | tf_op jit(solution)/shard_map/filter_rotate/pallas_call | solution.py:389
  154.7 0.7 reshape.42
  155.4 0.8 reshape.44
  156.2 0.1 copy.16
  156.3 0.7 reshape.45
  157.0 0.1 copy.15
  157.1 0.7 reshape.43
  157.8 0.0 copy-start
  157.8 4.8 %copy.21 = f32[128,8192]{1,0:T(8,128)} copy(f32[128,8192]{1,0:T(8,128)} %get-tuple-element.22) | data formatting | bytes 8388608
  162.5 0.0 copy-done
  162.5 0.0 copy-start.1
  162.5 2.0 %copy.22 = f32[128,8192]{1,0:T(8,128)} copy(f32[128,8192]{1,0:T(8,128)S(1)} %copy-done) | data formatting | bytes 8388608
  164.5 0.0 copy-done.1
  164.5 0.5 copy.23
Async XLA Ops:
  157.8 4.8 %copy-start = (f32[128,8192]{1,0:T(8,128)S(1)}, f32[128,8192]{1,0:T(8,128)}, u32[]{:S(2)}) copy-start(f32[128,8192]{1,0:T(8,128)} %get-tuple-element.23) | copy-start | bytes 12582916
  162.5 2.0 %copy-start.1 = (f32[1,128]{1,0:T(1,128)S(1)}, f32[1,128]{1,0:T(1,128)}, u32[]{:S(2)}) copy-start(f32[1,128]{1,0:T(1,128)} %get-tuple-element.14) | copy-start | bytes 1540

commit v2 on v1

--- a/solution.py
+++ b/solution.py
@@ -50,15 +50,15 @@
 
 def kernel(
     n_ob, n_pt,
-    cut_ref, pot_hbm, orb_hbm, eig_ref,
-    gram_out, hamil_out, ritz_out, rot_hbm, res_hbm,
-    ext, spare, coef, pot, shifts, zbuf, appl, filt_all, appl_all, est, rot, rota,
+    cut_ref, pot_hbm, orb_hbm, eig_hbm,
+    gram_out, hamil_out, ritz_out, rot, rota,
+    eig, ext, spare, coef, pot, shifts, zbuf, appl, filt_all, appl_all, est,
     quot, quot_in, part, part_in,
-    load_sem, pot_sem, zsend, zrecv, psend, precv, qsend, qrecv, gsend, grecv, out_sem,
+    load_sem, pot_sem, eig_sem, zsend, zrecv, psend, precv, qsend, qrecv, gsend, grecv,
 ):
     waves = ext.shape[0]
     outer, peers, n_dev = n_ob // 2, 2 * n_pt, n_ob * n_pt
-    norb = eig_ref.shape[1]
+    norb = eig.shape[1]
     ppl = G // outer
     n_plane, _, n_sub = filt_all.shape[:3]
     per_plane = SUBS // n_sub
@@ -74,9 +74,18 @@
     half = group // max(1, outer // 2)
     mirrored = half * (outer - 1 - group) + (1 - half) * group
 
-    def other_group(i):
-        t = outer - 1 - i - (i + mirrored + 1) // outer
+    def other_group(i, ends, middles):
+        if outer == 4:
+            t = ends[i] + mirrored * (middles[i] - ends[i])
+        else:
+            t = outer - 1 - i - (i + mirrored + 1) // outer
         return half * (outer - 1 - t) + (1 - half) * t
+
+    def target(i):
+        return other_group(i, (3, 2, 1), (2, 3, 0))
+
+    def source(i):
+        return other_group(i, (3, 1, 2), (3, 0, 2))
 
     barrier = pltpu.get_barrier_semaphore()
 
@@ -93,6 +102,11 @@
 
     def load_pot(b):
         return pltpu.make_async_copy(pot_hbm.at[:, :, b, :], pot.at[:, b], pot_sem.at[b])
+
+    def load_eig(w):
+        return pltpu.make_async_copy(
+            eig_hbm.at[:, w, :], eig.at[pl.ds(w * n_dev, n_dev)], eig_sem.at[w]
+        )
 
     for b in range(BLK):
         load(0, b).start()
@@ -101,6 +115,8 @@
     for w in range(1, waves):
         for b in range(BLK):
             load(w, b).start()
+    for w in range(waves):
+        load_eig(w).start()
     lax.fori_loop(1, n_dev, greet, 0)
 
     cut = cut_ref[0]
@@ -108,9 +124,6 @@
     half_width = 0.5 * (upper_bound - cut)
     inv = 1.0 / half_width
     shifts[...] = shift_matrix()
-    for w in range(waves):
-        hi, lo = split(eig_ref[pl.ds(w * n_dev, n_dev), :].T)
-        est[w] = jnp.concatenate([hi, lo, hi], axis=1)
     for b in range(BLK):
         load_pot(b).wait()
 
@@ -130,7 +143,7 @@
                 dst[x] = 0.5 * g if first else g - dst[x]
 
     def zcopy(w, i):
-        to = other_group(i)
+        to = target(i)
         return pltpu.make_async_remote_copy(
             src_ref=ext.at[w, pl.ds(to * ppl, ppl + 2)],
             dst_ref=zbuf.at[group, w],
@@ -139,6 +152,10 @@
             device_id=(to * 2 + ob % 2, pt),
             device_id_type=MESH,
         )
+
+    def send_wave(w):
+        for i in range(outer - 1):
+            zcopy(w, i).start()
 
     def zarrival(w, g):
         return pltpu.make_async_remote_copy(
@@ -204,13 +221,19 @@
         def _():
             pl.semaphore_wait(barrier, n_dev - 1)
 
-        for i in range(outer - 1):
-            zcopy(w, i).start()
+        @pl.when((w == 0) | (mirrored > 0))
+        def _():
+            send_wave(w)
+
         zbuf[group, w] = ext[w, pl.ds(group * ppl, ppl + 2)]
         process(w, group)
         return c
 
     lax.fori_loop(0, waves, filter_wave, 0)
+    for w in range(waves):
+        load_eig(w).wait()
+        hi, lo = split(eig[pl.ds(w * n_dev, n_dev), :].T)
+        est[w] = jnp.concatenate([hi, lo, hi], axis=1)
 
     def arrived(ref, w, sem):
         rows = ref.at[:, :, :, pl.ds(w * n_dev, n_dev), :]
@@ -255,19 +278,16 @@
 
     for w in range(waves):
 
-        def arrival(i, c, w=w):
-            g = other_group(i)
-            zarrival(w, g).wait_recv()
-            process(w, g)
-            return c
-
-        lax.fori_loop(0, outer - 1, arrival, 0)
+        for i in range(outer - 1):
+            with jax.named_scope(f"arr_{w}_{i}"):
+                zarrival(w, source(i)).wait_recv()
+            if i == outer - 2 and w < waves - 1:
+                pl.when(mirrored == 0)(functools.partial(send_wave, w + 1))
+            process(w, source(i))
         if w > 0:
             rotate(w - 1)
     num, den = rotate(waves - 1)
 
-    out_rot = pltpu.make_async_copy(rot, rot_hbm, out_sem.at[0])
-    out_rot.start()
     quot[...] = jnp.zeros_like(quot)
     quot[0, 0:1, :] = jnp.sum(num.T, axis=0, keepdims=True)
     quot[0, 1:2, :] = jnp.sum(den.T, axis=0, keepdims=True)
@@ -337,22 +357,27 @@
     ritz_out[...] = ritz
     column = jnp.broadcast_to(ritz, (LANES, norb)).T
 
-    n_cols = rot.shape[1] // LANES
-
-    def residual(t, c):
-        col = pl.ds(pl.multiple_of(t * LANES, LANES), LANES)
-        rota[:, col] = rota[:, col] - column * rot[:, col]
-        return c
-
-    lax.fori_loop(0, n_cols, residual, 0)
-    out_res = pltpu.make_async_copy(rota, res_hbm, out_sem.at[1])
-    out_res.start()
+    width = SUBS * LANES if rot.shape[1] % (SUBS * LANES) == 0 else LANES
+
+    def residual(k, c):
+        for t in range(width // LANES):
+            col = pl.ds(pl.multiple_of(k * width + t * LANES, LANES), LANES)
+            rota[:, col] = rota[:, col] - column * rot[:, col]
+        return c
+
+    lax.fori_loop(0, rot.shape[1] // width, residual, 0)
 
     def gfinish(k, total):
         gcopy(k).wait()
         return total + part_in[k]
 
     sums = lax.fori_loop(1, n_dev, gfinish, part[me]) / npts
+    row = lax.broadcasted_iota(jnp.int32, (norb, norb), 0)
+    col = lax.broadcasted_iota(jnp.int32, (norb, norb), 1)
+    place = jnp.where(row % n_dev * waves + row // n_dev == col, 1.0, 0.0)
+    sums = jnp.dot(
+        sums, place, precision=lax.Precision.HIGHEST, preferred_element_type=jnp.float32
+    )
     gram_out[...] = sums[:waves]
     hamil_out[...] = sums[waves : 2 * waves]
 
@@ -363,8 +388,27 @@
         for i, ref in enumerate((filt_all, appl_all)):
             rows = ref.at[:, :, :, pl.ds(0, share), :]
             pltpu.make_async_copy(rows, rows, psend.at[w, i]).wait()
-    out_rot.wait()
-    out_res.wait()
+
+
+def store_kernel(*refs):
+    n = (len(refs) - 1) // 2
+    copies = [pltpu.make_async_copy(refs[i], refs[n + i], refs[-1].at[i]) for i in range(n)]
+    for copy in copies:
+        copy.start()
+    for copy in copies:
+        copy.wait()
+
+
+def store(*arrays):
+    return pl.pallas_call(
+        store_kernel,
+        out_shape=tuple(jax.ShapeDtypeStruct(a.shape, a.dtype) for a in arrays),
+        in_specs=[pl.BlockSpec(memory_space=pltpu.VMEM)] * len(arrays),
+        out_specs=tuple([pl.BlockSpec(memory_space=pl.ANY)] * len(arrays)),
+        scratch_shapes=[pltpu.SemaphoreType.DMA((len(arrays),))],
+        compiler_params=pltpu.CompilerParams(vmem_limit_bytes=20 * 2**20),
+        name="store",
+    )(*arrays)
 
 
 def on_device(orbitals, potential, cutoff, eigvec):
@@ -379,12 +423,12 @@
     orb = orbitals.reshape(waves, tiles, LANES).transpose(1, 0, 2)
     orb = orb.reshape(G, SUBS, BLK * waves, LANES)
     pot = potential.reshape(G, SUBS, BLK, LANES)
-    eig = eigvec.reshape(n_dev, waves, norb).transpose(1, 0, 2).reshape(norb, norb)
+    eig = eigvec.reshape(n_dev, waves, norb)
     f32 = lambda *s: jax.ShapeDtypeStruct(s, jnp.float32)
     vm = lambda *s: pltpu.VMEM(s, jnp.float32)
     dma = pltpu.SemaphoreType.DMA
     vmem = pl.BlockSpec(memory_space=pltpu.VMEM)
-    anywhere = pl.BlockSpec(memory_space=pl.ANY)
+    hbm = pl.BlockSpec(memory_space=pltpu.HBM)
     padded = -(-2 * waves // SUBS) * SUBS
     gram, hamil, ritz, rotated, residual = pl.pallas_call(
         functools.partial(kernel, n_ob, n_pt),
@@ -392,9 +436,10 @@
             f32(waves, norb), f32(waves, norb), f32(1, norb),
             f32(norb, rows * LANES), f32(norb, rows * LANES),
         ),
-        in_specs=[pl.BlockSpec(memory_space=pltpu.SMEM), anywhere, anywhere, vmem],
-        out_specs=(vmem, vmem, vmem, anywhere, anywhere),
+        in_specs=[pl.BlockSpec(memory_space=pltpu.SMEM), hbm, hbm, hbm],
+        out_specs=(vmem,) * 5,
         scratch_shapes=[
+            vm(norb, norb),
             vm(waves, G + 2, BLK, SUBS, LANES),
             vm(G, BLK, SUBS, LANES),
             vm(G, BLK, SUBS, LANES),
@@ -405,25 +450,22 @@
             vm(n_plane, BLK, n_sub, norb, LANES),
             vm(n_plane, BLK, n_sub, norb, LANES),
             pltpu.VMEM((waves, norb, 3 * n_dev), jnp.bfloat16),
-            vm(norb, rows * LANES),
-            vm(norb, rows * LANES),
             vm(1, SUBS, norb),
             vm(n_dev, SUBS, norb),
             vm(n_dev, padded, norb),
             vm(n_dev, padded, norb),
-            dma((waves, BLK)), dma((BLK,)),
+            dma((waves, BLK)), dma((BLK,)), dma((waves,)),
             dma((waves, outer)), dma((waves, outer)),
             dma((waves, 2)), dma((waves, 2)),
             dma((n_dev,)), dma((n_dev,)), dma((n_dev,)), dma((n_dev,)),
-            dma((2,)),
         ],
         compiler_params=pltpu.CompilerParams(
-            collective_id=0, has_side_effects=True, vmem_limit_bytes=60 * 2**20
+            collective_id=0, has_side_effects=True, vmem_limit_bytes=44 * 2**20
         ),
         name="filter_rotate",
     )(cutoff, pot, orb, eig)
-    back = lambda m: m.reshape(waves, waves, n_dev).transpose(0, 2, 1).reshape(waves, norb)
-    return (back(gram), back(hamil), rotated, residual, ritz[0])
+    gram, hamil, rotated, residual, ritz = store(gram, hamil, rotated, residual, ritz)
+    return (gram, hamil, rotated, residual, ritz[0])
 
 
 def solution(mesh):

time: 165 us -> 144 us (0.87)
  Pallas kernels: 152 us -> 140 us
  local copies, waits for them, and re-layouts: 11.9 us -> 2.06 us
    pallas_call x1, Pallas kernels: 152 us -> 137 us  [on_device(): pl.pallas_call(functools.partial(kernel, n_ob, n_pt), out_shape=(f32(wave...]
    unnamed x7 -> x4, local copies, waits for them, and re-layouts: 7.29 us -> 2.06 us
    reshape x7 -> x0, local copies, waits for them, and re-layouts: 4.57 us -> none  [the longest x6 3.09 us: on_device(): m.reshape(waves, waves, n_dev).transpose(0, 2, 1).reshape(waves, norb)]
    pallas_call x0 -> x1, Pallas kernels: none -> 3.45 us  [store(): pl.pallas_call(store_kernel, out_shape=tuple((jax.ShapeDtypeStruct(a.shap...]
where the time goes in v2:
time: 144 us
  Pallas kernels  140 us (97%)
  local copies, waits for them, and re-layouts  2.06 us (1%)
    pallas_call x1, Pallas kernels, on_device(): pl.pallas_call(functools.partial(kernel, n_ob, n_pt), out_shape=(f32(wave...  137 us
    pallas_call x1, Pallas kernels, store(): pl.pallas_call(store_kernel, out_shape=tuple((jax.ShapeDtypeStruct(a.shap...  3.45 us

profile of v2, /device:TPU:0, one launch (start us, length us, event | category | flops | bytes accessed | tf_op | source)
XLA Modules:
  0.0 143.5 jit_solution(2882977701912920937)
XLA Ops:
  1.3 0.0 copy-start
  1.3 1.2 copy-done
  2.5 0.0 copy-start.1
  2.5 0.8 copy-done.1
  3.3 136.7 %filter_rotate.1 = (f32[4,128]{1,0:T(4,128)S(1)}, f32[4,128]{1,0:T(4,128)S(1)}, f32[1,128]{1,0:T(1,128)S(1)}, f32[128,8192]{1,0:T(8,128)S(1)}, f32[128,8192]{1,0:T(8,128)S(1)}) custom-call(f32[1]{0:T(128)S(6)} %copy.10.cut_ref, f32[64,8,4,128]{3,2,1,0:T(4,128)S(1)} %bitcast.8, f32[64,8,16,128]{3,2,1,0:T(8,128)} %bitcast.10, f32[32,4,128]{2,1,0:T(4,128)S(1)} %bitcast.9), custom_call_target="tpu_custom_call" | custom-call | tf_op jit(solution)/shard_map/filter_rotate/pallas_call | solution.py:433
  140.1 3.5 %store.1 = (f32[4,128]{1,0:T(4,128)}, f32[4,128]{1,0:T(4,128)}, f32[128,8192]{1,0:T(8,128)}, f32[128,8192]{1,0:T(8,128)}, f32[1,128]{1,0:T(1,128)}) custom-call(f32[4,128]{1,0:T(4,128)S(1)} %get-tuple-element.15.refs_0_, f32[4,128]{1,0:T(4,128)S(1)} %get-tuple-element.16.refs_1_, f32[128,8192]{1,0:T(8,128)S(1)} %get-tuple-element.17.refs_2_, ...), custom_call_target="tpu_custom_call" | custom-call | tf_op jit(solution)/shard_map/store/pallas_call | solution.py:403
Async XLA Ops:
  1.3 1.2 copy-start
  2.5 0.8 copy-start.1

commit v3 on v2

--- a/solution.py
+++ b/solution.py
@@ -109,9 +109,9 @@
         )
 
     for b in range(BLK):
+        load_pot(b).start()
+    for b in range(BLK):
         load(0, b).start()
-    for b in range(BLK):
-        load_pot(b).start()
     for w in range(1, waves):
         for b in range(BLK):
             load(w, b).start()
@@ -239,11 +239,9 @@
         rows = ref.at[:, :, :, pl.ds(w * n_dev, n_dev), :]
         return pltpu.make_async_copy(rows, rows, sem)
 
-    num = den = None
-
-    def rotate(w):
-        for i, ref in enumerate((filt_all, appl_all)):
-            arrived(ref, w, precv.at[w, i]).wait()
+    def rotate(w, which):
+        for i in which:
+            arrived((filt_all, appl_all)[i], w, precv.at[w, i]).wait()
         last = w == waves - 1
         rows = pl.ds(w * n_dev, n_dev)
 
@@ -252,32 +250,29 @@
             for h in range(n_sub // 2):
                 pair = (2 * h, 2 * h + 1)
                 f = jnp.concatenate(
-                    [ref[p, b, s, rows, :] for ref in (filt_all, appl_all) for s in pair], axis=1
+                    [(filt_all, appl_all)[i][p, b, s, rows, :] for i in which for s in pair],
+                    axis=1,
                 )
                 hi, lo = split(f)
                 out = jnp.dot(
                     est[w], jnp.concatenate([hi, hi, lo], axis=0), preferred_element_type=jnp.float32
                 )
-                for j, s in enumerate(pair):
-                    col = pl.ds(
-                        pl.multiple_of((p * n_sub * BLK + s * BLK + b) * LANES, LANES), LANES
-                    )
-                    x = out[:, j * LANES : (j + 1) * LANES]
-                    y = out[:, (2 + j) * LANES : (3 + j) * LANES]
+                for n, (i, s) in enumerate((i, s) for i in which for s in pair):
+                    first = pl.multiple_of((p * n_sub * BLK + s * BLK + b) * LANES, LANES)
+                    col = pl.ds(first, LANES)
+                    ref = (rot, rota)[i]
+                    x = out[:, n * LANES : (n + 1) * LANES]
                     if w > 0:
-                        x += rot[:, col]
-                        y += rota[:, col]
-                    rot[:, col] = x
-                    rota[:, col] = y
+                        x += ref[:, col]
+                    ref[:, col] = x
                     if last:
-                        c = (c[0] + x * y, c[1] + x * x)
+                        c += x * (x if i == 0 else rot[:, col])
             return c
 
         zero = jnp.zeros((norb, LANES), jnp.float32)
-        return lax.fori_loop(0, n_plane * BLK, body, (zero, zero) if last else 0)
+        return lax.fori_loop(0, n_plane * BLK, body, zero if last else 0)
 
     for w in range(waves):
-
         for i in range(outer - 1):
             with jax.named_scope(f"arr_{w}_{i}"):
                 zarrival(w, source(i)).wait_recv()
@@ -285,8 +280,9 @@
                 pl.when(mirrored == 0)(functools.partial(send_wave, w + 1))
             process(w, source(i))
         if w > 0:
-            rotate(w - 1)
-    num, den = rotate(waves - 1)
+            rotate(w - 1, (0, 1))
+    den = rotate(waves - 1, (0,))
+    num = rotate(waves - 1, (1,))
 
     quot[...] = jnp.zeros_like(quot)
     quot[0, 0:1, :] = jnp.sum(num.T, axis=0, keepdims=True)
@@ -424,6 +420,7 @@
     orb = orb.reshape(G, SUBS, BLK * waves, LANES)
     pot = potential.reshape(G, SUBS, BLK, LANES)
     eig = eigvec.reshape(n_dev, waves, norb)
+    pot, eig = (pltpu.with_memory_space_constraint(a, pltpu.HBM) for a in (pot, eig))
     f32 = lambda *s: jax.ShapeDtypeStruct(s, jnp.float32)
     vm = lambda *s: pltpu.VMEM(s, jnp.float32)
     dma = pltpu.SemaphoreType.DMA

time: 144 us -> 141 us (0.979)
  local copies, waits for them, and re-layouts: 2.06 us -> 0 us
    unnamed x4 -> x0, local copies, waits for them, and re-layouts: 2.06 us -> none
where the time goes in v3:
time: 141 us
  Pallas kernels  139 us (99%)
    pallas_call x1, Pallas kernels, on_device(): pl.pallas_call(functools.partial(kernel, n_ob, n_pt), out_shape=(f32(wave...  136 us
    pallas_call x1, Pallas kernels, store(): pl.pallas_call(store_kernel, out_shape=tuple((jax.ShapeDtypeStruct(a.shap...  3.45 us

profile of v3, /device:TPU:0, one launch (start us, length us, event | category | flops | bytes accessed | tf_op | source)
XLA Modules:
  0.0 140.7 jit_solution(1580692870310646854)
XLA Ops:
  1.3 135.9 %filter_rotate.1 = (f32[4,128]{1,0:T(4,128)S(1)}, f32[4,128]{1,0:T(4,128)S(1)}, f32[1,128]{1,0:T(1,128)S(1)}, f32[128,8192]{1,0:T(8,128)S(1)}, f32[128,8192]{1,0:T(8,128)S(1)}) custom-call(f32[1]{0:T(128)S(6)} %copy.10.cut_ref, f32[64,8,4,128]{3,2,1,0:T(4,128)} %bitcast.9, f32[64,8,16,128]{3,2,1,0:T(8,128)} %bitcast.8, f32[32,4,128]{2,1,0:T(4,128)} %bitcast.10), custom_call_target="tpu_custom_call" | custom-call | tf_op jit(solution)/shard_map/filter_rotate/pallas_call | solution.py:430
  137.2 3.5 %store.1 = (f32[4,128]{1,0:T(4,128)}, f32[4,128]{1,0:T(4,128)}, f32[128,8192]{1,0:T(8,128)}, f32[128,8192]{1,0:T(8,128)}, f32[1,128]{1,0:T(1,128)}) custom-call(f32[4,128]{1,0:T(4,128)S(1)} %get-tuple-element.15.refs_0_, f32[4,128]{1,0:T(4,128)S(1)} %get-tuple-element.16.refs_1_, f32[128,8192]{1,0:T(8,128)S(1)} %get-tuple-element.17.refs_2_, ...), custom_call_target="tpu_custom_call" | custom-call | tf_op jit(solution)/shard_map/store/pallas_call | solution.py:399

commit v4 on v3

--- a/solution.py
+++ b/solution.py
@@ -14,6 +14,7 @@
 ROWS = G * G // LANES
 BLK = ROWS // SUBS
 CHUNK = 16
+PARTS = 8
 MESH = pl.DeviceIdType.MESH
 upper_bound = 8.0
 quot_eps = 1e-06
@@ -127,11 +128,12 @@
     for b in range(BLK):
         load_pot(b).wait()
 
-    def prep(x, c):
-        coef[x] = (2.0 * inv) * (pot[x] + (3.0 - center))
-        return c
-
-    lax.fori_loop(0, G, prep, 0)
+    def prep(q, c):
+        planes = pl.ds(q * CHUNK, CHUNK)
+        coef[planes] = (2.0 * inv) * (pot[planes] + (3.0 - center))
+        return c
+
+    lax.fori_loop(0, G // CHUNK, prep, 0)
 
     def sweep(cur, dst, first):
         for q in range(G // CHUNK):
@@ -282,11 +284,11 @@
         if w > 0:
             rotate(w - 1, (0, 1))
     den = rotate(waves - 1, (0,))
+    quot[...] = jnp.zeros_like(quot)
+    quot[0, 1:2, :] = jnp.sum(den.T, axis=0, keepdims=True)
     num = rotate(waves - 1, (1,))
 
-    quot[...] = jnp.zeros_like(quot)
     quot[0, 0:1, :] = jnp.sum(num.T, axis=0, keepdims=True)
-    quot[0, 1:2, :] = jnp.sum(den.T, axis=0, keepdims=True)
 
     def qcopy(k):
         return pltpu.make_async_remote_copy(
@@ -388,7 +390,17 @@
 
 def store_kernel(*refs):
     n = (len(refs) - 1) // 2
-    copies = [pltpu.make_async_copy(refs[i], refs[n + i], refs[-1].at[i]) for i in range(n)]
+    copies = []
+    for i in range(n):
+        rows = refs[i].shape[0]
+        step = max(SUBS, rows // PARTS)
+        for k, first in enumerate(range(0, rows, step)):
+            part = pl.ds(first, min(step, rows - first))
+            copies.append(
+                pltpu.make_async_copy(
+                    refs[i].at[part], refs[n + i].at[part], refs[-1].at[i, k]
+                )
+            )
     for copy in copies:
         copy.start()
     for copy in copies:
@@ -401,7 +413,7 @@
         out_shape=tuple(jax.ShapeDtypeStruct(a.shape, a.dtype) for a in arrays),
         in_specs=[pl.BlockSpec(memory_space=pltpu.VMEM)] * len(arrays),
         out_specs=tuple([pl.BlockSpec(memory_space=pl.ANY)] * len(arrays)),
-        scratch_shapes=[pltpu.SemaphoreType.DMA((len(arrays),))],
+        scratch_shapes=[pltpu.SemaphoreType.DMA((len(arrays), PARTS))],
         compiler_params=pltpu.CompilerParams(vmem_limit_bytes=20 * 2**20),
         name="store",
     )(*arrays)

time: 141 us -> 141 us (level)
  no operation moved by 1% of the time
where the time goes in v4:
time: 141 us
  Pallas kernels  140 us (99%)
    pallas_call x1, Pallas kernels, on_device(): pl.pallas_call(functools.partial(kernel, n_ob, n_pt), out_shape=(f32(wave...  136 us
    pallas_call x1, Pallas kernels, store(): pl.pallas_call(store_kernel, out_shape=tuple((jax.ShapeDtypeStruct(a.shap...  3.64 us

profile of v4, /device:TPU:0, one launch (start us, length us, event | category | flops | bytes accessed | tf_op | source)
XLA Modules:
  0.0 140.9 jit_solution(6905745978780437884)
XLA Ops:
  1.3 136.0 %filter_rotate.1 = (f32[4,128]{1,0:T(4,128)S(1)}, f32[4,128]{1,0:T(4,128)S(1)}, f32[1,128]{1,0:T(1,128)S(1)}, f32[128,8192]{1,0:T(8,128)S(1)}, f32[128,8192]{1,0:T(8,128)S(1)}) custom-call(f32[1]{0:T(128)S(6)} %copy.10.cut_ref, f32[64,8,4,128]{3,2,1,0:T(4,128)} %bitcast.9, f32[64,8,16,128]{3,2,1,0:T(8,128)} %bitcast.8, f32[32,4,128]{2,1,0:T(4,128)} %bitcast.10), custom_call_target="tpu_custom_call" | custom-call | tf_op jit(solution)/shard_map/filter_rotate/pallas_call | solution.py:442
  137.3 3.6 %store.1 = (f32[4,128]{1,0:T(4,128)}, f32[4,128]{1,0:T(4,128)}, f32[128,8192]{1,0:T(8,128)}, f32[128,8192]{1,0:T(8,128)}, f32[1,128]{1,0:T(1,128)}) custom-call(f32[4,128]{1,0:T(4,128)S(1)} %get-tuple-element.15.refs_0_, f32[4,128]{1,0:T(4,128)S(1)} %get-tuple-element.16.refs_1_, f32[128,8192]{1,0:T(8,128)S(1)} %get-tuple-element.17.refs_2_, ...), custom_call_target="tpu_custom_call" | custom-call | tf_op jit(solution)/shard_map/store/pallas_call | solution.py:411
